TPU v7x, 32 devices: a whole 2x2x4 slice. The times are simulated.
32 devices in a mesh: dp: 4 (over x, core), cls: 8 (over z, y).
Axes of the slice: x: 2, y: 2, z: 4, core: 2. Of those that a mesh axis runs over, the one named last changes fastest.
Arguments:
- pooled: bfloat16 [4096, 512], P(('dp', 'cls')), may hold values from -6 to 6
- proj: bfloat16 [512, 512], replicated, may hold values from -0.25 to 0.25
- centers: bfloat16 [2048, 512], P('cls'), may hold values from -6 to 6
- labels: int32 [4096], P(('dp', 'cls')), may hold values from 0 to 2047
- row_weight: bfloat16 [4096], P(('dp', 'cls')), may hold values from 0.5 to 2
Outputs:
- row_loss: float32 [4096], P(('dp', 'cls'))
- center_grad: float32 [2048, 512], P('cls')
- proj_grad: float32 [512, 512], replicated
All inputs are finite; a program needn't handle non-finite values.
Results may differ from a plain program's by a relative error of at most 0.005.
Values may be sent and summed in bfloat16 or wider, within the bound.
No kernel may reach another device: no remote copies, remote signals or barrier semaphores. Data moves between devices by JAX's collectives and lax.ppermute only.
A program may use at most 128 MiB of HBM per device.

v0:
```python
import math
import jax
import jax.numpy as jnp
from jax import lax
from jax.sharding import PartitionSpec as P

SCALE = 64.0
MARGIN = 0.35
EPS = 1e-06


def unit_rows(values):
    inverse = lax.rsqrt(jnp.sum(values * values, axis=1, keepdims=True) + EPS)
    return ((values * inverse).astype(jnp.bfloat16), inverse)


def onehot_of(lab_block, width):
    columns = jnp.arange(width, dtype=jnp.int32)
    return (lab_block[:, None] == columns[None, :]).astype(jnp.float32)


def split_product(feat_rows, grad_hidden):
    upper = grad_hidden.astype(jnp.bfloat16)
    lower = (grad_hidden - upper.astype(jnp.float32)).astype(jnp.bfloat16)
    dims = (((0,), (0,)), ((), ()))
    first = lax.dot_general(feat_rows, upper, dims, preferred_element_type=jnp.float32)
    second = lax.dot_general(feat_rows, lower, dims, preferred_element_type=jnp.float32)
    return first + second


def on_device(pooled, proj, centers, labels, row_weight):
    rows = pooled.shape[0]
    c_dev = centers.shape[0]
    width = centers.shape[1]
    shard = lax.axis_index("cls")
    unit, c_inv = unit_rows(centers.astype(jnp.float32))
    label_all = lax.all_gather(labels, "cls", axis=0, tiled=True) - shard * c_dev
    feat_all, weight_all = (
        lax.all_gather(pooled, "cls", axis=0, tiled=True),
        lax.all_gather(row_weight, "cls", axis=0, tiled=True),
    )
    hidden = jnp.dot(feat_all, proj, preferred_element_type=jnp.float32)
    emb_all, z_inv = unit_rows(hidden)
    total_rows = emb_all.shape[0]
    block = math.gcd(total_rows, 1024)
    count = total_rows // block
    emb_blocks = emb_all.reshape(count, block, width)
    lab_blocks = label_all.reshape(count, block)

    def stats_step(carry, pieces):
        emb_block, lab_block = pieces
        cosine = lax.dot_general(
            emb_block, unit, (((1,), (1,)), ((), ())), preferred_element_type=jnp.float32
        )
        onehot = onehot_of(lab_block, c_dev)
        logits = SCALE * cosine - SCALE * MARGIN * onehot
        expo = jnp.exp(logits)
        return (carry, (expo, jnp.sum(expo, axis=1), jnp.sum(logits * onehot, axis=1)))

    _, (expo_blocks, part_total, part_target) = lax.scan(
        stats_step, jnp.zeros((), jnp.float32), (emb_blocks, lab_blocks)
    )
    total, target = lax.psum(
        (part_total.reshape(total_rows), part_target.reshape(total_rows)), "cls"
    )
    loss_all = jnp.log(total) - target

    def grad_step(accum, pieces):
        emb_block, lab_block, expo_block, total_block, weight_block = pieces
        onehot = onehot_of(lab_block, c_dev)
        grad_block = (weight_block[:, None] * (expo_block / total_block[:, None] - onehot)).astype(
            jnp.bfloat16
        )
        accum = accum + SCALE * lax.dot_general(
            grad_block, emb_block, (((0,), (0,)), ((), ())), preferred_element_type=jnp.float32
        )
        return (accum, grad_block)

    grad_unit, grad_blocks = lax.scan(
        grad_step,
        jnp.zeros((c_dev, width), jnp.float32),
        (
            emb_blocks,
            lab_blocks,
            expo_blocks,
            total.reshape(count, block),
            weight_all.astype(jnp.float32).reshape(count, block),
        ),
    )
    grad_logits = grad_blocks.reshape(total_rows, c_dev)
    grad_unit = lax.psum(grad_unit, "dp")
    unit_f = unit.astype(jnp.float32)
    center_grad = c_inv * (grad_unit - unit_f * jnp.sum(unit_f * grad_unit, axis=1, keepdims=True))
    grad_emb = SCALE * jnp.dot(grad_logits, unit, preferred_element_type=jnp.float32)
    row_loss = lax.dynamic_slice_in_dim(loss_all, shard * rows, rows)
    emb_f = emb_all.astype(jnp.float32)
    grad_hidden = z_inv * (grad_emb - emb_f * jnp.sum(emb_f * grad_emb, axis=1, keepdims=True))
    proj_part = split_product(feat_all, grad_hidden)
    proj_grad = lax.psum(proj_part, ("dp", "cls"))
    return (row_loss, center_grad, proj_grad)


def solution(mesh):
    in_specs = (P(("dp", "cls"), None), P(), P("cls", None), P(("dp", "cls")), P(("dp", "cls")))
    out_specs = (P(("dp", "cls")), P("cls", None), P())
    return jax.shard_map(
        on_device, mesh=mesh, in_specs=in_specs, out_specs=out_specs, check_vma=False
    )
```

profile of v0, /device:TPU:0, one launch (start us, length us, event | category | flops | bytes accessed | tf_op | source)
XLA Modules:
  0.0 259.5 jit_solution(14060492183931136996)
XLA Ops:
  7.2 0.0 copy-start
  7.2 0.0 all-gather.4.cloned.1.call-start
  7.2 0.7 all-gather.4.cloned.1.call-update
  7.9 0.0 all-reduce.4.cloned.1.call-start
  8.0 22.5 %all-gather.1 = bf16[8,1,128]{2,1,0:T(2,128)(2,1)S(1)} all-gather(bf16[1,1,128]{2,1,0:T(2,128)(2,1)} %bitcast.20), channel_id=1, replica_groups=mesh['dp'=4,'cls'=8] {'cls'}, dimensions={0}, use_global_device_ids=true | all-gather | bytes 2304 | tf_op jit(solution)/shard_map/all_gather | solution.py:40
  30.4 16.6 %all-gather = s32[8,1,128]{2,1,0:T(1,128)S(1)} all-gather(s32[1,1,128]{2,1,0:T(1,128)} %bitcast.21), channel_id=1, replica_groups=mesh['dp'=4,'cls'=8] {'cls'}, dimensions={0}, use_global_device_ids=true | all-gather | bytes 4608 | tf_op jit(solution)/shard_map/all_gather | solution.py:37
  47.0 1.1 fusion.14
  48.2 5.0 %all-gather.4.cloned.1.call-done = bf16[1024,512]{1,0:T(8,128)(2,1)} async-done(((bf16[128,512]{1,0:T(8,128)(2,1)}), bf16[1024,512]{1,0:T(8,128)(2,1)}) %all-gather.4.cloned.1.call-update) | async-done | bytes 1048592 | tf_op jit(solution)/shard_map/all_gather | solution.py:39
  53.1 0.0 copy-done
  53.1 2.0 multiply_reduce_fusion
  55.1 0.0 copy-start.3
  55.1 0.3 multiply_convert_fusion
  55.4 0.7 copy-done.3
  56.1 1.6 exponential_reduce_fusion
  57.7 19.4 %all-reduce = (f32[1024]{0:T(1024)S(1)}, f32[1024]{0:T(1024)S(1)}) all-reduce(f32[1024]{0:T(1024)S(1)} %get-tuple-element.47, f32[1024]{0:T(1024)S(1)} %get-tuple-element.46), channel_id=1, replica_groups=mesh['dp'=4,'cls'=8] {'cls'}, use_global_device_ids=true, to_apply=%region_5.6 | all-reduce | flops 2048 | bytes 16384 | tf_op jit(solution)/shard_map/psum | solution.py:63
  77.1 2.5 convolution_multiply_fusion.1
  79.6 0.0 copy-start.1
  79.6 3.3 %fusion = (f32[1024]{0:T(1024)S(1)}, f32[1024,512]{0,1:T(8,128)}) fusion(bf16[1024,512]{0,1:T(8,128)(2,1)S(1)} %multiply_convert_fusion, bf16[256,512]{1,0:T(8,128)(2,1)S(1)} %copy-done.3, f32[256]{0:T(256)S(1)} %add_rsqrt_fusion.1, f32[1024,256]{0,1:T(8,128)} %get-tuple-element.60, f32[1024]{0:T(1024)S(1)} %get-tuple-element.49, f32[1024]{0:T(1024)S(1)} %bitcast.16, ...), kind=kOutput, calls=%fused_computation.2 | convolution fusion | flops 272497664 | bytes 4473856 | tf_op jit(solution)/shard_map/dot_general | solution.py:94
  82.9 0.0 all-reduce.4.cloned.1.call-update
  83.0 0.0 all-reduce.6.cloned.1.call-start
  83.0 0.0 copy-done.1
  83.0 0.0 copy-start.2
  83.0 2.5 fusion.6
  85.5 0.0 copy-done.2
  85.5 1.7 fusion.3
  87.3 0.0 all-reduce.6.cloned.1.call-update
  87.3 0.6 dynamic_slice.21
  87.9 25.9 %all-reduce.4.cloned.1.call-done = f32[256,512]{1,0:T(8,128)} async-done(((f32[256,512]{1,0:T(8,128)}), f32[256,512]{1,0:T(8,128)}) %all-reduce.4.cloned.1.call-update) | async-done | bytes 524304 | tf_op jit(solution)/shard_map/psum | solution.py:91
  113.7 1.2 fusion.16
  115.0 2.0 fusion.18
  117.0 133.4 %all-reduce.6.cloned.1.call-done = f32[512,512]{0,1:T(8,128)} async-done(((f32[512,512]{0,1:T(8,128)}), f32[512,512]{0,1:T(8,128)}) %all-reduce.6.cloned.1.call-update) | async-done | bytes 1048592 | tf_op jit(solution)/shard_map/psum | solution.py:99
  250.4 2.5 copy.9
  (5 shorter events, 0.0 us)
Async XLA Ops:
  7.2 46.0 %copy-start = (bf16[512,512]{1,0:T(8,128)(2,1)S(1)}, bf16[512,512]{1,0:T(8,128)(2,1)}, u32[]{:S(2)}) copy-start(bf16[512,512]{1,0:T(8,128)(2,1)} %param.6) | copy-start | bytes 1572868
  7.2 45.9 %all-gather.4.cloned.1.call-start = ((), (), s32[]{:S(2)}) async-start(), calls=%async_computation | async-start | bytes 1179648 | tf_op jit(solution)/shard_map/all_gather | solution.py:39
  7.9 105.8 %all-reduce.4.cloned.1.call-start = ((), (), s32[]{:S(2)}) async-start(), calls=%async_computation.1 | async-start | bytes 1048576 | tf_op jit(solution)/shard_map/psum | solution.py:91
  55.1 1.0 copy-start.3
  79.6 3.4 %copy-start.1 = (bf16[1024,512]{1,0:T(8,128)(2,1)S(1)}, bf16[1024,512]{1,0:T(8,128)(2,1)}, u32[]{:S(2)}) copy-start(bf16[1024,512]{1,0:T(8,128)(2,1)} %all-gather.4.cloned.1.call-done) | copy-start | bytes 3145732
  83.0 167.4 %all-reduce.6.cloned.1.call-start = ((), (), s32[]{:S(2)}) async-start(), calls=%async_computation.2 | async-start | bytes 2097152 | tf_op jit(solution)/shard_map/psum | solution.py:99
  83.0 2.5 copy-start.2
Sparse Core Ops, SparseCore 0:
  10.1 42.9 all-gather.3
  83.1 30.5 all-reduce.3
  119.5 130.8 all-reduce.5
where the time goes:
time: 260 us; the launch traced here: 259 us
  waiting for transfers between devices  165 us (63%)
  blocking collectives  58.4 us (22%)
  between operations  13.8 us (5%)
  matrix products  13.7 us (5%)
  other arithmetic  4.62 us (2%)
  local copies, waits for them, and re-layouts  3.81 us (1%)
    psum x1, waiting for transfers between devices, on_device(): proj_grad = lax.psum(proj_part, ('dp', 'cls'))  133 us
    psum x1, waiting for transfers between devices, on_device(): grad_unit = lax.psum(grad_unit, 'dp')  25.9 us
    all_gather x1, blocking collectives, on_device(): lax.all_gather(row_weight, 'cls', axis=0, tiled=True)  22.5 us
    psum x1, blocking collectives, on_device(): lax.psum((part_total.reshape(total_rows), part_target.reshape(total_rows)...  19.4 us
    all_gather x1, blocking collectives, on_device(): lax.all_gather(labels, 'cls', axis=0, tiled=True) - shard * c_dev  16.6 us
  transfers between devices with their start and end apart: 3, of which 3 were waited for; matrix products, arithmetic and copies ran while one was open for 4% of the time, Pallas kernels for 0%

commit v1 on v0

--- a/solution.py
+++ b/solution.py
@@ -88,7 +88,7 @@
         ),
     )
     grad_logits = grad_blocks.reshape(total_rows, c_dev)
-    grad_unit = lax.psum(grad_unit, "dp")
+    grad_unit = jnp.sum(lax.all_gather(grad_unit, "dp"), axis=0)
     unit_f = unit.astype(jnp.float32)
     center_grad = c_inv * (grad_unit - unit_f * jnp.sum(unit_f * grad_unit, axis=1, keepdims=True))
     grad_emb = SCALE * jnp.dot(grad_logits, unit, preferred_element_type=jnp.float32)

time: 260 us -> 242 us (0.931)
  waiting for transfers between devices: 165 us -> 153 us
  matrix products: 13.7 us -> 7.09 us
    psum x1 -> x0, waiting for transfers between devices: 25.9 us -> none  [on_device(): grad_unit = lax.psum(grad_unit, 'dp')]
    all_gather x0 -> x1, waiting for transfers between devices: none -> 21.2 us  [on_device(): grad_unit = jnp.sum(lax.all_gather(grad_unit, 'dp'), axis=0)]
    psum x1, waiting for transfers between devices: 133 us -> 126 us  [on_device(): proj_grad = lax.psum(proj_part, ('dp', 'cls'))]
    dot_general x1, matrix products: 3.33 us -> 0.68 us  [on_device(): jnp.dot(grad_logits, unit, preferred_element_type=jnp.float32)]
  transfers between devices with their start and end apart: 3 -> 3, of which waited for: 3 -> 3; matrix products, arithmetic and copies ran while one was open for 4% -> 2% of each run, Pallas kernels for 0% -> 0%
where the time goes in v1:
time: 242 us; the launch traced here: 241 us
  waiting for transfers between devices  153 us (63%)
  blocking collectives  58.5 us (24%)
  between operations  13.8 us (6%)
  matrix products  7.09 us (3%)
  other arithmetic  4.42 us (2%)
  local copies, waits for them, and re-layouts  4.33 us (2%)
    psum x1, waiting for transfers between devices, on_device(): proj_grad = lax.psum(proj_part, ('dp', 'cls'))  126 us
    all_gather x1, blocking collectives, on_device(): lax.all_gather(row_weight, 'cls', axis=0, tiled=True)  22.5 us
    all_gather x1, waiting for transfers between devices, on_device(): grad_unit = jnp.sum(lax.all_gather(grad_unit, 'dp'), axis=0)  21.2 us
    psum x1, blocking collectives, on_device(): lax.psum((part_total.reshape(total_rows), part_target.reshape(total_rows)...  19.4 us
    all_gather x1, blocking collectives, on_device(): lax.all_gather(labels, 'cls', axis=0, tiled=True) - shard * c_dev  16.6 us
    all_gather x1, waiting for transfers between devices, on_device(): lax.all_gather(pooled, 'cls', axis=0, tiled=True)  4.98 us
  transfers between devices with their start and end apart: 3, of which 3 were waited for; matrix products, arithmetic and copies ran while one was open for 2% of the time, Pallas kernels for 0%

profile of v1, /device:TPU:0, one launch (start us, length us, event | category | flops | bytes accessed | tf_op | source)
XLA Modules:
  0.0 241.2 jit_solution(9374848905410918199)
XLA Ops:
  7.2 0.0 copy-start
  7.2 0.0 all-gather.6.cloned.1.call-start
  7.2 0.7 all-gather.6.cloned.1.call-update
  7.9 0.0 all-reduce.3.cloned.1.call-start
  8.0 22.5 %all-gather.2 = bf16[8,1,128]{2,1,0:T(2,128)(2,1)S(1)} all-gather(bf16[1,1,128]{2,1,0:T(2,128)(2,1)} %bitcast.22), channel_id=1, replica_groups=mesh['dp'=4,'cls'=8] {'cls'}, dimensions={0}, use_global_device_ids=true | all-gather | bytes 2304 | tf_op jit(solution)/shard_map/all_gather | solution.py:40
  30.4 16.6 %all-gather.1 = s32[8,1,128]{2,1,0:T(1,128)S(1)} all-gather(s32[1,1,128]{2,1,0:T(1,128)} %bitcast.23), channel_id=1, replica_groups=mesh['dp'=4,'cls'=8] {'cls'}, dimensions={0}, use_global_device_ids=true | all-gather | bytes 4608 | tf_op jit(solution)/shard_map/all_gather | solution.py:37
  47.0 1.1 fusion.14
  48.2 5.0 %all-gather.6.cloned.1.call-done = bf16[1024,512]{1,0:T(8,128)(2,1)} async-done(((bf16[128,512]{1,0:T(8,128)(2,1)}), bf16[1024,512]{1,0:T(8,128)(2,1)}) %all-gather.6.cloned.1.call-update) | async-done | bytes 1048592 | tf_op jit(solution)/shard_map/all_gather | solution.py:39
  53.1 0.0 copy-done
  53.1 2.0 multiply_reduce_fusion
  55.1 0.0 copy-start.2
  55.2 0.3 multiply_convert_fusion
  55.4 0.7 copy-done.2
  56.1 0.7 exponential_reduce_fusion
  56.7 19.4 %all-reduce = (f32[1024]{0:T(1024)S(1)}, f32[1024]{0:T(1024)S(1)}) all-reduce(f32[1024]{0:T(1024)S(1)} %get-tuple-element.47, f32[1024]{0:T(1024)S(1)} %get-tuple-element.46), channel_id=1, replica_groups=mesh['dp'=4,'cls'=8] {'cls'}, use_global_device_ids=true, to_apply=%region_5.6 | all-reduce | flops 2048 | bytes 16384 | tf_op jit(solution)/shard_map/psum | solution.py:63
  76.2 0.0 copy-start.1
  76.2 0.7 fusion
  76.9 0.5 copy-done.1
  77.4 0.8 fusion.6
  78.2 1.7 fusion.3
  79.9 0.0 all-reduce.3.cloned.1.call-update
  79.9 0.0 all-gather.8.cloned.1.call-start
  79.9 1.3 convolution_multiply_fusion.1
  81.2 0.0 all-gather.8.cloned.1.call-update
  81.3 0.6 dynamic_slice.21
  81.9 126.0 %all-reduce.3.cloned.1.call-done = f32[512,512]{0,1:T(8,128)} async-done(((f32[512,512]{0,1:T(8,128)}), f32[512,512]{0,1:T(8,128)}) %all-reduce.3.cloned.1.call-update) | async-done | bytes 1048592 | tf_op jit(solution)/shard_map/psum | solution.py:99
  207.9 2.5 %copy.9 = f32[512,512]{1,0:T(8,128)} copy(f32[512,512]{0,1:T(8,128)} %all-reduce.3.cloned.1.call-done) | data formatting | bytes 2097152
  210.4 21.2 %all-gather.8.cloned.1.call-done = f32[1024,512]{1,0:T(8,128)} async-done(((f32[256,512]{1,0:T(8,128)}), f32[1024,512]{1,0:T(8,128)}) %all-gather.8.cloned.1.call-update) | async-done | bytes 2097168 | tf_op jit(solution)/shard_map/all_gather | solution.py:91
  231.6 1.9 reduce_sum.69
  233.4 0.2 fusion.16
  233.7 1.0 fusion.18
  (5 shorter events, 0.0 us)
Async XLA Ops:
  7.2 46.0 %copy-start = (bf16[512,512]{1,0:T(8,128)(2,1)S(1)}, bf16[512,512]{1,0:T(8,128)(2,1)}, u32[]{:S(2)}) copy-start(bf16[512,512]{1,0:T(8,128)(2,1)} %param.6) | copy-start | bytes 1572868
  7.2 46.0 %all-gather.6.cloned.1.call-start = ((), (), s32[]{:S(2)}) async-start(), calls=%async_computation | async-start | bytes 1179648 | tf_op jit(solution)/shard_map/all_gather | solution.py:39
  7.9 200.0 %all-reduce.3.cloned.1.call-start = ((), (), s32[]{:S(2)}) async-start(), calls=%async_computation.1 | async-start | bytes 2097152 | tf_op jit(solution)/shard_map/psum | solution.py:99
  55.1 1.0 copy-start.2
  76.2 1.2 copy-start.1
  79.9 151.7 %all-gather.8.cloned.1.call-start = ((), (), s32[]{:S(2)}) async-start(), calls=%async_computation.2 | async-start | bytes 2621440 | tf_op jit(solution)/shard_map/all_gather | solution.py:91
Sparse Core Ops, SparseCore 0:
  10.1 42.9 all-gather.5
  80.0 127.8 all-reduce.2
  210.0 21.4 all-gather.7
